TPU v7x, 32 devices: a whole 2x2x4 slice. The times are simulated.
32 devices in a mesh: batch: 4 (over y, core), seq: 8 (over z, x).
Axes of the slice: x: 2, y: 2, z: 4, core: 2. Of those that a mesh axis runs over, the one named last changes fastest.
Arguments:
- tokens: bfloat16 [4, 1024, 1024], P('batch', 'seq'), may hold values from -6 to 6
- w_query: bfloat16 [512, 512], replicated, may hold values from -0.25 to 0.25
- w_value: bfloat16 [512, 512], replicated, may hold values from -0.25 to 0.25
- w_out: bfloat16 [512, 512], replicated, may hold values from -0.25 to 0.25
- long_filter: float32 [512, 1024], P('seq'), may hold values from -0.1875 to 0.1875
- cotangent: bfloat16 [4, 1024, 1024], P('batch', 'seq'), may hold values from -6 to 6
Outputs:
- block_out: bfloat16 [4, 1024, 1024], P('batch', 'seq')
- grad_tokens: bfloat16 [4, 1024, 1024], P('batch', 'seq')
- grad_query: float32 [512, 512], P('seq')
- grad_value: float32 [512, 512], P('seq')
- grad_out: float32 [512, 512], P('seq')
- grad_filter: float32 [512, 1024], P('seq')
All inputs are finite; a program needn't handle non-finite values.
Results may differ from a plain program's by a relative error of at most 0.017.
Values may be sent and summed in bfloat16 or wider, within the bound.
A program may use at most 64 MiB of HBM per device.

v0:
```python
import math
import jax
import jax.numpy as jnp
from jax import lax
from jax.sharding import PartitionSpec as P

precise = lax.Precision.HIGH


def swapped(x, axis, stride):
    return lax.ppermute(x, axis, [(i, i ^ 1 << stride) for i in range(lax.axis_size(axis))])


def angle_tables(count_rows, count_cols, period):
    left = lax.broadcasted_iota(jnp.int32, (count_rows, count_cols), 0)
    right = lax.broadcasted_iota(jnp.int32, (count_rows, count_cols), 1)
    turns = left * right % period
    angle = turns.astype(jnp.float32) * (2.0 * math.pi / period)
    return (jnp.cos(angle), jnp.sin(angle))


def rotation(cosines, sines, direction):
    upper = jnp.stack([cosines, direction * sines])
    lower_row = jnp.stack([-direction * sines, cosines])
    return jnp.stack([upper, lower_row])


def split_sizes(length):
    period = 2 * length
    first = 1 << (period.bit_length() - 1 + 1) // 2
    return (first, period // first)


def make_tables(first, second):
    cos_first, sin_first = angle_tables(first, first, first)
    cos_twist, sin_twist = angle_tables(first, second, first * second)
    cos_second, sin_second = angle_tables(second, second, second)
    forward_first = rotation(cos_first, sin_first, 1.0)
    inverse_first = rotation(cos_first, sin_first, -1.0)
    forward_second = rotation(cos_second, sin_second, 1.0)
    inverse_second = rotation(cos_second, sin_second, -1.0)
    return (forward_first, inverse_first, forward_second, inverse_second, cos_twist, sin_twist)


def forward_spectrum(signal, tables, first, second):
    forward_first, inverse_first, forward_second, inverse_second, cos_twist, sin_twist = tables
    lower = first // 2
    folded = signal.reshape(2, signal.shape[1], lower, second)
    section = jnp.einsum("brnm,abnk->arkm", folded, forward_first[:, :, :lower], precision=precise)
    turned = jnp.stack(
        [
            section[0] * cos_twist + section[1] * sin_twist,
            section[1] * cos_twist - section[0] * sin_twist,
        ]
    )
    return jnp.einsum("brkm,abmj->arkj", turned, forward_second, precision=precise)


def inverse_spectrum(spectrum, tables, first, second, both):
    forward_first, inverse_first, forward_second, inverse_second, cos_twist, sin_twist = tables
    lower = first // 2
    rows = spectrum.shape[1]
    inner = jnp.einsum("brkj,abjm->arkm", spectrum, inverse_second, precision=precise)
    turned = jnp.stack(
        [inner[0] * cos_twist - inner[1] * sin_twist, inner[1] * cos_twist + inner[0] * sin_twist]
    )
    if both:
        signal = jnp.einsum(
            "brkm,abkn->arnm", turned, inverse_first[:, :, :, :lower], precision=precise
        )
        return (signal / (first * second)).reshape(2, rows, lower * second)
    signal = jnp.einsum("brkm,bkn->rnm", turned, inverse_first[0][:, :, :lower], precision=precise)
    return (signal / (first * second)).reshape(rows, lower * second)


def complex_product(left, right):
    return jnp.stack(
        [left[0] * right[0] - left[1] * right[1], left[0] * right[1] + left[1] * right[0]]
    )


def conjugate_product(left, right):
    return jnp.stack(
        [left[0] * right[0] + left[1] * right[1], left[0] * right[1] - left[1] * right[0]]
    )


def mirror(array, seq_dim):
    moved = array
    for bit_index in range(lax.axis_size("seq").bit_length() - 1):
        moved = swapped(moved, "seq", bit_index)
    return jnp.flip(moved, axis=seq_dim)


def to_channels(stacked):
    return lax.all_to_all(stacked, "seq", split_axis=1, concat_axis=2, tiled=True)


def to_tokens(stacked):
    return lax.all_to_all(stacked, "seq", split_axis=2, concat_axis=1, tiled=True)


def body(tokens, w_query, w_value, w_out, long_filter, cotangent):
    floats = jnp.float32
    halves = jnp.bfloat16
    half = w_query.shape[0]
    seq_count = lax.axis_size("seq")
    batch_count = lax.axis_size("batch")
    length = tokens.shape[1] * seq_count
    first, second = split_sizes(length)
    tables = make_tables(first, second)
    scale = (2.0 * batch_count * length) ** (-0.5)
    source = tokens[0]
    front = source[:, :half]
    back = source[:, half:]
    back_strand = mirror(back, 0)[:, ::-1]
    strands = jnp.stack([front, back_strand])
    query = jnp.einsum("stk,kh->sht", strands, w_query, preferred_element_type=floats).astype(
        halves
    )
    value = jnp.einsum("stk,kh->sht", strands, w_value, preferred_element_type=floats).astype(
        halves
    )
    value_sig = to_channels(value).astype(floats)
    value_spec = forward_spectrum(value_sig, tables, first, second)
    taps_spec = forward_spectrum(
        jnp.stack([long_filter, jnp.zeros_like(long_filter)]), tables, first, second
    )
    conv_sig = inverse_spectrum(complex_product(value_spec, taps_spec), tables, first, second, True)
    conv_tok = to_tokens(conv_sig.astype(halves))
    gated = (query.astype(floats) * conv_tok.astype(floats)).astype(halves)
    gated_back = mirror(gated[1], 1)
    out_front = jnp.einsum("ht,hk->tk", gated[0], w_out, preferred_element_type=floats)
    out_back = jnp.einsum("ht,hk->tk", gated_back, w_out, preferred_element_type=floats)
    block_out = jnp.concatenate(
        [front.astype(floats) + out_front, back.astype(floats) + out_back[:, ::-1]], axis=1
    ).astype(halves)[None]
    upstream = cotangent[0]
    up_front = upstream[:, :half]
    up_back = upstream[:, half:]
    grad_back = mirror(up_back, 0)[:, ::-1]
    grad_strands = jnp.stack([up_front, grad_back])
    grad_gated = jnp.einsum(
        "stk,hk->sht", grad_strands, w_out, preferred_element_type=floats
    ).astype(halves)
    grad_query_t = (grad_gated.astype(floats) * conv_tok.astype(floats)).astype(halves)
    grad_conv = (grad_gated.astype(floats) * query.astype(floats)).astype(halves)
    grad_sig = to_channels(grad_conv).astype(floats)
    grad_spec = forward_spectrum(grad_sig, tables, first, second)
    value_grad_sig = inverse_spectrum(
        conjugate_product(taps_spec, grad_spec), tables, first, second, True
    )
    filter_part = (
        inverse_spectrum(conjugate_product(value_spec, grad_spec), tables, first, second, False)
        * scale
    )
    grad_value_t = to_tokens(value_grad_sig.astype(halves))
    front_in = jnp.einsum(
        "ht,kh->tk", grad_query_t[0], w_query, preferred_element_type=floats
    ) + jnp.einsum("ht,kh->tk", grad_value_t[0], w_value, preferred_element_type=floats)
    paired = jnp.stack([grad_query_t[1], grad_value_t[1]])
    paired = mirror(paired, 2)
    back_in = jnp.einsum(
        "ht,kh->tk", paired[0], w_query, preferred_element_type=floats
    ) + jnp.einsum("ht,kh->tk", paired[1], w_value, preferred_element_type=floats)
    grad_tokens = jnp.concatenate(
        [up_front.astype(floats) + front_in, up_back.astype(floats) + back_in[:, ::-1]], axis=1
    ).astype(halves)[None]
    term_query = jnp.einsum("stk,sht->kh", strands, grad_query_t, preferred_element_type=floats)
    term_value = jnp.einsum("stk,sht->kh", strands, grad_value_t, preferred_element_type=floats)
    term_out = jnp.einsum("sht,stk->hk", gated, grad_strands, preferred_element_type=floats)
    share = lax.psum_scatter(
        jnp.concatenate([term_query, term_value, term_out], axis=1) * scale,
        "seq",
        scatter_dimension=0,
        tiled=True,
    )
    share, filter_total = (
        lax.psum(share.astype(jnp.bfloat16), "batch").astype(jnp.float32),
        lax.psum(filter_part.astype(jnp.bfloat16), "batch").astype(jnp.float32),
    )
    return (
        block_out,
        grad_tokens,
        share[:, :half],
        share[:, half : 2 * half],
        share[:, 2 * half :],
        filter_total,
    )


def solution(mesh):
    in_specs = (P("batch", "seq", None), P(), P(), P(), P("seq", None), P("batch", "seq", None))
    out_specs = (
        P("batch", "seq", None),
        P("batch", "seq", None),
        P("seq", None),
        P("seq", None),
        P("seq", None),
        P("seq", None),
    )
    return jax.shard_map(body, mesh=mesh, in_specs=in_specs, out_specs=out_specs, check_vma=False)
```

profile of v0, /device:TPU:0, one launch (start us, length us, event | category | flops | bytes accessed | tf_op | source)
XLA Modules:
  0.0 290.6 jit_solution(196216083540338696)
XLA Ops:
  7.2 1.0 slice_bitcast_fusion.6
  8.2 3.0 %collective-permute-start = (bf16[128,512]{1,0:T(8,128)(2,1)S(1)}, bf16[128,512]{1,0:T(8,128)(2,1)S(1)}, u32[]{:S(2)}, u32[]{:S(2)}) collective-permute-start(bf16[128,512]{1,0:T(8,128)(2,1)S(1)} %get-tuple-element.64), channel_id=1, source_target_pairs={{0,1},{1,0},{2,3},{3,2},{4,5},{5,4},{6,7},{7,6},{8,9},{9,8},{10,11... | collective-permute-start | bytes 393224 | tf_op jit(solution)/shard_map/ppermute | solution.py:11
  12.4 2.8 collective-permute-done
  15.2 2.0 collective-permute-start.1
  17.6 1.8 collective-permute-start.7
  19.4 1.4 collective-permute-done.1
  20.8 3.2 %collective-permute-start.2 = (bf16[128,512]{1,0:T(8,128)(2,1)S(1)}, bf16[128,512]{1,0:T(8,128)(2,1)S(1)}, u32[]{:S(2)}, u32[]{:S(2)}) collective-permute-start(bf16[128,512]{1,0:T(8,128)(2,1)S(1)} %collective-permute-done.1), channel_id=1, source_target_pairs={{0,4},{1,5},{2,6},{3,7},{4,0},{5,1},{6,2},{7,3},{8,12},{9,13},{10,... | collective-permute-start | bytes 393224 | tf_op jit(solution)/shard_map/ppermute | solution.py:11
  24.3 2.4 collective-permute-start.8
  26.8 6.2 %collective-permute-done.2 = bf16[128,512]{1,0:T(8,128)(2,1)S(1)} collective-permute-done((bf16[128,512]{1,0:T(8,128)(2,1)S(1)}, bf16[128,512]{1,0:T(8,128)(2,1)S(1)}, u32[]{:S(2)}, u32[]{:S(2)}) %collective-permute-start.2) | collective-permute-done | bytes 131104 | tf_op jit(solution)/shard_map/ppermute | solution.py:11
  33.4 1.3 fusion.63
  35.3 1.1 multiply_convert_fusion
  37.3 5.2 %all-to-all-start.2 = ((bf16[2,512,128]{2,0,1:T(2,128)(2,1)}), bf16[2,512,128]{2,0,1:T(2,128)(2,1)S(1)}, u32[]{:S(2)}, u32[]{:S(2)}) async-start(bf16[2,512,128]{2,0,1:T(2,128)(2,1)} %copy.140), calls=%async_computation.2 | async-start | bytes 524288 | tf_op jit(solution)/shard_map/all_to_all | solution.py:96
  44.5 6.3 %all-to-all-done.2 = bf16[2,512,128]{2,0,1:T(2,128)(2,1)S(1)} async-done(((bf16[2,512,128]{2,0,1:T(2,128)(2,1)}), bf16[2,512,128]{2,0,1:T(2,128)(2,1)S(1)}, u32[]{:S(2)}, u32[]{:S(2)}) %all-to-all-start.2) | async-done | bytes 262176 | tf_op jit(solution)/shard_map/all_to_all | solution.py:96
  50.8 4.2 %all-to-all-start = ((bf16[2,512,128]{2,0,1:T(2,128)(2,1)}), bf16[2,512,128]{2,0,1:T(2,128)(2,1)}, u32[]{:S(2)}, u32[]{:S(2)}) async-start(bf16[2,512,128]{2,0,1:T(2,128)(2,1)} %copy.122), calls=%async_computation | async-start | bytes 524288 | tf_op jit(solution)/shard_map/all_to_all | solution.py:96
  56.7 1.5 convolution_bitcast_fusion
  58.9 2.0 copy.142
  60.9 3.1 %convolution_bitcast_fusion.1 = f32[2,64,64,32]{1,2,3,0:T(8,128)} fusion(bf16[2,64,32,32]{1,3,2,0:T(8,128)(2,1)} %bitcast.316, f32[1,2,64,64]{3,2,1,0:T(8,128)S(1)} %get-tuple-element.66, f32[1,2,64,64]{3,2,1,0:T(8,128)S(1)} %get-tuple-element.77), kind=kOutput, calls=%fused_computation.41 | convolution fusion | flops 100671488 | bytes 1376256 | tf_op jit(solution)/shard_map/brnm,abnk->arkm/dot_general | solution.py:49
  64.0 1.7 copy.123
  65.7 2.0 copy.124
  67.7 1.9 convolution_bitcast_fusion.2
  69.6 2.6 multiply_add_fusion.4
  72.4 2.7 copy.129
  75.2 1.7 pad_maximum_fusion.3
  76.9 2.7 copy.144
  79.6 2.8 fusion.28
  82.4 1.1 fusion.34
  85.0 2.4 fusion.37
  87.3 3.3 %copy.146 = f32[2,32,64,64]{2,3,1,0:T(8,128)} copy(f32[2,32,64,64]{3,1,2,0:T(8,128)} %fusion.37) | data formatting | bytes 2097152 | tf_op jit(solution)/shard_map/brkj,abjm->arkm/dot_general | solution.py:63
  90.7 3.2 %pad_maximum_fusion = f32[2,64,64,32]{1,2,3,0:T(8,128)} fusion(f32[1,64,64,32]{1,2,3,0:T(8,128)} %get-tuple-element.75, f32[1,64,64,32]{1,2,3,0:T(8,128)} %get-tuple-element.76), kind=kLoop, calls=%fused_computation.1 | loop fusion | flops 262144 | bytes 2097152 | tf_op jit(solution)/shard_map/stack | solution.py:50
  93.9 3.8 %copy.126 = f32[2,64,64,32]{2,3,0,1:T(8,128)} copy(f32[2,64,64,32]{1,2,3,0:T(8,128)} %pad_maximum_fusion) | data formatting | bytes 2097152 | tf_op jit(solution)/shard_map/stack | solution.py:50
  97.7 2.8 fusion.25
  100.5 2.1 multiply_add_fusion.1
  102.7 1.0 fusion.31
  103.7 2.2 copy.131
  105.9 2.6 fusion.40
  108.5 2.3 copy.160
  110.8 4.4 %multiply_subtract_fusion = (f32[1,64,64,32]{1,2,3,0:T(8,128)S(1)}, f32[1,64,64,32]{1,2,3,0:T(8,128)}, f32[1,64,64,32]{1,2,3,0:T(8,128)S(1)}, f32[1,64,64,32]{1,...) fusion(f32[2,64,64,32]{1,2,3,0:T(8,128)} %bitcast.299, f32[64,32]{0,1:T(8,128)S(1)} %get-tuple-element.89, ...), kind=kLoop, calls=%fused_computation.77 | loop fusion | flops 2359296 | bytes 6307840 | tf_op jit(solution)/shard_map/sub | solution.py:65
  116.1 1.3 copy.239
  117.5 2.1 reshape.296
  119.6 5.7 %all-to-all-start.3 = ((bf16[8,2,8192]{2,1,0:T(2,128)(2,1)}), bf16[8,2,8192]{2,1,0:T(2,128)(2,1)}, u32[]{:S(2)}, u32[]{:S(2)}) async-start(bf16[8,2,8192]{2,1,0:T(2,128)(2,1)} %reshape.296), calls=%async_computation.3 | async-start | bytes 524288 | tf_op jit(solution)/shard_map/all_to_all | solution.py:100
  125.3 1.9 fusion.52
  128.0 1.1 reshape.294
  129.1 4.5 %all-to-all-done.3 = bf16[8,2,8192]{2,1,0:T(2,128)(2,1)} async-done(((bf16[8,2,8192]{2,1,0:T(2,128)(2,1)}), bf16[8,2,8192]{2,1,0:T(2,128)(2,1)}, u32[]{:S(2)}, u32[]{:S(2)}) %all-to-all-start.3) | async-done | bytes 262176 | tf_op jit(solution)/shard_map/all_to_all | solution.py:100
  133.7 4.1 %all-to-all-start.1 = ((bf16[8,2,8192]{2,1,0:T(2,128)(2,1)}), bf16[8,2,8192]{2,1,0:T(2,128)(2,1)}, u32[]{:S(2)}, u32[]{:S(2)}) async-start(bf16[8,2,8192]{2,1,0:T(2,128)(2,1)} %reshape.294), calls=%async_computation.1 | async-start | bytes 524288 | tf_op jit(solution)/shard_map/all_to_all | solution.py:100
  137.8 1.3 reshape.297
  139.8 1.3 convolution_bitcast_fusion.3
  141.1 4.8 %all-to-all-done.1 = bf16[8,2,8192]{2,1,0:T(2,128)(2,1)} async-done(((bf16[8,2,8192]{2,1,0:T(2,128)(2,1)}), bf16[8,2,8192]{2,1,0:T(2,128)(2,1)}, u32[]{:S(2)}, u32[]{:S(2)}) %all-to-all-start.1) | async-done | bytes 262176 | tf_op jit(solution)/shard_map/all_to_all | solution.py:100
  146.0 1.3 reshape.295
  147.9 1.0 copy.138
  148.9 1.4 multiply_convert_fusion.1
  150.4 1.4 convolution_bitcast_fusion.4
  152.2 2.1 maximum_multiply_fusion
  154.3 3.5 %copy.204 = f32[512,1536]{1,0:T(8,128)} copy(f32[512,1536]{0,1:T(8,128)} %maximum_multiply_fusion) | data formatting | bytes 6291456
  158.5 1.9 fusion.65
  161.9 2.1 collective-permute-start.3
  164.3 9.5 %collective-permute-done.3 = bf16[512,128]{0,1:T(8,128)(2,1)S(1)} collective-permute-done((bf16[512,128]{0,1:T(8,128)(2,1)S(1)}, bf16[512,128]{0,1:T(8,128)(2,1)S(1)}, u32[]{:S(2)}, u32[]{:S(2)}) %collective-permute-start.3) | collective-permute-done | bytes 131104 | tf_op jit(solution)/shard_map/ppermute | solution.py:11
  174.2 13.3 %collective-permute-done.4 = bf16[512,128]{0,1:T(8,128)(2,1)S(1)} collective-permute-done((bf16[512,128]{0,1:T(8,128)(2,1)S(1)}, bf16[512,128]{0,1:T(8,128)(2,1)S(1)}, u32[]{:S(2)}, u32[]{:S(2)}) %collective-permute-start.4) | collective-permute-done | bytes 131104 | tf_op jit(solution)/shard_map/ppermute | solution.py:11
  188.0 16.3 %collective-permute-done.5 = bf16[512,128]{0,1:T(8,128)(2,1)S(1)} collective-permute-done((bf16[512,128]{0,1:T(8,128)(2,1)S(1)}, bf16[512,128]{0,1:T(8,128)(2,1)S(1)}, u32[]{:S(2)}, u32[]{:S(2)}) %collective-permute-start.5) | collective-permute-done | bytes 131104 | tf_op jit(solution)/shard_map/ppermute | solution.py:11
  205.0 1.2 collective-permute-start.11
  207.0 7.8 %collective-permute-done.11 = bf16[2,512,128]{1,2,0:T(8,128)(2,1)S(1)} collective-permute-done((bf16[2,512,128]{1,2,0:T(8,128)(2,1)S(1)}, bf16[2,512,128]{1,2,0:T(8,128)(2,1)S(1)}, u32[]{:S(2)}, u32[]{:S(2)}) %collective-permute-start.11) | collective-permute-done | bytes 262176 | tf_op jit(solution)/shard_map/ppermute | solution.py:11
  216.3 27.5 %reduce-scatter.4.cloned.1.call-done = f32[64,1536]{1,0:T(8,128)} async-done(((f32[512,1536]{1,0:T(8,128)}), f32[64,1536]{1,0:T(8,128)}) %reduce-scatter.4.cloned.1.call-update) | async-done | bytes 393232
  243.8 1.9 copy.205
  246.5 33.0 %all-reduce.4.cloned.1.call-done = (bf16[64,1536]{0,1:T(8,128)(2,1)}, bf16[64,1024]{0,1:T(8,128)(2,1)}) async-done(((bf16[64,1536]{0,1:T(8,128)(2,1)}, bf16[64,1024]{0,1:T(8,128)(2,1)}), (bf16[64,1536]{0,1:T(8,128)(2,1)}, bf16[64,1024]{0,1:T(8,128)(2,1)})) %all-reduce.4.cloned.1.call-update) | async-done | bytes 327696 | tf_op jit(solution)/shard_map/psum | solution.py:179
  279.5 1.1 fusion.141
  (136 shorter events, 23.1 us)
Async XLA Ops:
  7.2 28.1 %copy-start = (bf16[512,512]{1,0:T(8,128)(2,1)S(1)}, bf16[512,512]{1,0:T(8,128)(2,1)}, u32[]{:S(2)}) copy-start(bf16[512,512]{1,0:T(8,128)(2,1)} %param.9) | copy-start | bytes 1572868
  8.2 131.6 %copy-start.9 = (bf16[1,128,512]{2,1,0:T(8,128)(2,1)}, bf16[1,128,512]{2,1,0:T(8,128)(2,1)S(1)}, u32[]{:S(2)}) copy-start(bf16[1,128,512]{2,1,0:T(8,128)(2,1)S(1)} %get-tuple-element.63) | copy-start | bytes 393220
  8.2 6.9 %collective-permute-start = (bf16[128,512]{1,0:T(8,128)(2,1)S(1)}, bf16[128,512]{1,0:T(8,128)(2,1)S(1)}, u32[]{:S(2)}, u32[]{:S(2)}) collective-permute-start(bf16[128,512]{1,0:T(8,128)(2,1)S(1)} %get-tuple-element.64), channel_id=1, source_target_pairs={{0,1},{1,0},{2,3},{3,2},{4,5},{5,4},{6,7},{7,6},{8,9},{9,8},{10,11... | collective-permute-start | bytes 393224 | tf_op jit(solution)/shard_map/ppermute | solution.py:11
  12.3 25.0 %copy-start.14 = (bf16[1,128,512]{2,1,0:T(8,128)(2,1)}, bf16[1,128,512]{2,1,0:T(8,128)(2,1)S(1)}, u32[]{:S(2)}) copy-start(bf16[1,128,512]{2,1,0:T(8,128)(2,1)S(1)} %get-tuple-element.61) | copy-start | bytes 393220
  12.3 5.3 %collective-permute-start.6 = (bf16[128,512]{1,0:T(8,128)(2,1)S(1)}, bf16[128,512]{1,0:T(8,128)(2,1)S(1)}, u32[]{:S(2)}, u32[]{:S(2)}) collective-permute-start(bf16[128,512]{1,0:T(8,128)(2,1)S(1)} %get-tuple-element.62), channel_id=1, source_target_pairs={{0,1},{1,0},{2,3},{3,2},{4,5},{5,4},{6,7},{7,6},{8,9},{9,8},{10,11... | collective-permute-start | bytes 393224 | tf_op jit(solution)/shard_map/ppermute | solution.py:11
  15.2 5.6 %collective-permute-start.1 = (bf16[128,512]{1,0:T(8,128)(2,1)S(1)}, bf16[128,512]{1,0:T(8,128)(2,1)S(1)}, u32[]{:S(2)}, u32[]{:S(2)}) collective-permute-start(bf16[128,512]{1,0:T(8,128)(2,1)S(1)} %collective-permute-done), channel_id=1, source_target_pairs={{0,2},{1,3},{2,0},{3,1},{4,6},{5,7},{6,4},{7,5},{8,10},{9,11},{10,... | collective-permute-start | bytes 393224 | tf_op jit(solution)/shard_map/ppermute | solution.py:11
  17.3 38.7 %copy-start.25 = (f32[1,64,64]{2,1,0:T(8,128)}, f32[1,64,64]{2,1,0:T(8,128)S(1)}, u32[]{:S(2)}) copy-start(f32[1,64,64]{2,1,0:T(8,128)S(1)} %fusion.120) | copy-start | bytes 49156
  17.6 6.8 %collective-permute-start.7 = (bf16[128,512]{1,0:T(8,128)(2,1)S(1)}, bf16[128,512]{1,0:T(8,128)(2,1)S(1)}, u32[]{:S(2)}, u32[]{:S(2)}) collective-permute-start(bf16[128,512]{1,0:T(8,128)(2,1)S(1)} %collective-permute-done.6), channel_id=1, source_target_pairs={{0,2},{1,3},{2,0},{3,1},{4,6},{5,7},{6,4},{7,5},{8,10},{9,11},{10,... | collective-permute-start | bytes 393224 | tf_op jit(solution)/shard_map/ppermute | solution.py:11
  20.8 12.2 %collective-permute-start.2 = (bf16[128,512]{1,0:T(8,128)(2,1)S(1)}, bf16[128,512]{1,0:T(8,128)(2,1)S(1)}, u32[]{:S(2)}, u32[]{:S(2)}) collective-permute-start(bf16[128,512]{1,0:T(8,128)(2,1)S(1)} %collective-permute-done.1), channel_id=1, source_target_pairs={{0,4},{1,5},{2,6},{3,7},{4,0},{5,1},{6,2},{7,3},{8,12},{9,13},{10,... | collective-permute-start | bytes 393224 | tf_op jit(solution)/shard_map/ppermute | solution.py:11
  24.2 31.8 %copy-start.27 = (f32[1,64,64]{2,1,0:T(8,128)}, f32[1,64,64]{2,1,0:T(8,128)S(1)}, u32[]{:S(2)}) copy-start(f32[1,64,64]{2,1,0:T(8,128)S(1)} %get-tuple-element.87) | copy-start | bytes 49156
  24.3 10.5 %collective-permute-start.8 = (bf16[128,512]{1,0:T(8,128)(2,1)S(1)}, bf16[128,512]{1,0:T(8,128)(2,1)S(1)}, u32[]{:S(2)}, u32[]{:S(2)}) collective-permute-start(bf16[128,512]{1,0:T(8,128)(2,1)S(1)} %collective-permute-done.7), channel_id=1, source_target_pairs={{0,4},{1,5},{2,6},{3,7},{4,0},{5,1},{6,2},{7,3},{8,12},{9,13},{10,... | collective-permute-start | bytes 393224 | tf_op jit(solution)/shard_map/ppermute | solution.py:11
  34.8 8.5 %copy-start.11 = (bf16[512,512]{1,0:T(8,128)(2,1)S(1)}, bf16[512,512]{1,0:T(8,128)(2,1)}, u32[]{:S(2)}) copy-start(bf16[512,512]{1,0:T(8,128)(2,1)} %param.8) | copy-start | bytes 1572868
  35.3 8.3 %copy-start.13 = (bf16[128,512]{1,0:T(8,128)(2,1)}, bf16[128,512]{1,0:T(8,128)(2,1)S(1)}, u32[]{:S(2)}) copy-start(bf16[128,512]{1,0:T(8,128)(2,1)S(1)} %rev.24) | copy-start | bytes 393220
  36.4 19.3 %copy-start.29 = (f32[64,1024]{1,0:T(8,128)S(1)}, f32[64,1024]{1,0:T(8,128)}, u32[]{:S(2)}) copy-start(f32[64,1024]{1,0:T(8,128)} %param.10) | copy-start | bytes 786436
  37.3 13.5 %all-to-all-start.2 = ((bf16[2,512,128]{2,0,1:T(2,128)(2,1)}), bf16[2,512,128]{2,0,1:T(2,128)(2,1)S(1)}, u32[]{:S(2)}, u32[]{:S(2)}) async-start(bf16[2,512,128]{2,0,1:T(2,128)(2,1)} %copy.140), calls=%async_computation.2 | async-start | bytes 524288 | tf_op jit(solution)/shard_map/all_to_all | solution.py:96
  50.8 5.9 %copy-start.17 = (bf16[2,512,128]{2,0,1:T(2,128)(2,1)}, bf16[2,512,128]{2,0,1:T(2,128)(2,1)S(1)}, u32[]{:S(2)}) copy-start(bf16[2,512,128]{2,0,1:T(2,128)(2,1)S(1)} %all-to-all-done.2) | copy-start | bytes 786436
  50.8 13.2 %all-to-all-start = ((bf16[2,512,128]{2,0,1:T(2,128)(2,1)}), bf16[2,512,128]{2,0,1:T(2,128)(2,1)}, u32[]{:S(2)}, u32[]{:S(2)}) async-start(bf16[2,512,128]{2,0,1:T(2,128)(2,1)} %copy.122), calls=%async_computation | async-start | bytes 524288 | tf_op jit(solution)/shard_map/all_to_all | solution.py:96
  56.7 1.5 copy-start.18
  67.7 2.0 copy-start.4
  67.7 2.0 copy-start.31
  76.9 2.8 copy-start.23
  76.9 2.8 copy-start.24
  79.6 2.8 copy-start.3
  83.5 1.4 copy-start.1
  83.6 1.4 copy-start.21
  83.6 1.4 copy-start.22
  97.7 2.8 copy-start.2
  110.8 4.4 %copy-start.19 = (f32[1,2,64,64]{3,2,1,0:T(8,128)S(1)}, f32[1,2,64,64]{3,2,1,0:T(8,128)}, u32[]{:S(2)}) copy-start(f32[1,2,64,64]{3,2,1,0:T(8,128)} %get-tuple-element.65) | copy-start | bytes 98308
  110.8 4.4 %copy-start.20 = (f32[1,2,64,64]{3,2,1,0:T(8,128)S(1)}, f32[1,2,64,64]{3,2,1,0:T(8,128)}, u32[]{:S(2)}) copy-start(f32[1,2,64,64]{3,2,1,0:T(8,128)} %get-tuple-element.78) | copy-start | bytes 98308
  119.6 14.1 %all-to-all-start.3 = ((bf16[8,2,8192]{2,1,0:T(2,128)(2,1)}), bf16[8,2,8192]{2,1,0:T(2,128)(2,1)}, u32[]{:S(2)}, u32[]{:S(2)}) async-start(bf16[8,2,8192]{2,1,0:T(2,128)(2,1)} %reshape.296), calls=%async_computation.3 | async-start | bytes 524288 | tf_op jit(solution)/shard_map/all_to_all | solution.py:100
  133.7 12.3 %all-to-all-start.1 = ((bf16[8,2,8192]{2,1,0:T(2,128)(2,1)}), bf16[8,2,8192]{2,1,0:T(2,128)(2,1)}, u32[]{:S(2)}, u32[]{:S(2)}) async-start(bf16[8,2,8192]{2,1,0:T(2,128)(2,1)} %reshape.294), calls=%async_computation.1 | async-start | bytes 524288 | tf_op jit(solution)/shard_map/all_to_all | solution.py:100
  137.7 106.0 %reduce-scatter.4.cloned.1.call-start = ((), (), s32[]{:S(2)}) async-start(), calls=%async_computation.5 | async-start | bytes 3538944
  148.9 2.9 copy-start.10
  150.4 1.4 copy-start.7
  150.4 1.8 copy-start.6
  157.8 0.8 copy-start.26
  157.8 0.8 copy-start.28
  157.8 3.7 %copy-start.8 = (bf16[2,512,128]{1,2,0:T(8,128)(2,1)S(1)}, bf16[2,512,128]{1,2,0:T(8,128)(2,1)}, u32[]{:S(2)}) copy-start(bf16[2,512,128]{1,2,0:T(8,128)(2,1)} %copy-done.7) | copy-start | bytes 786436
  157.8 121.7 %all-reduce.4.cloned.1.call-start = ((), (), s32[]{:S(2)}) async-start(), calls=%async_computation.6 | async-start | bytes 1310720 | tf_op jit(solution)/shard_map/psum | solution.py:179
  160.4 3.5 %copy-start.5 = (bf16[512,512]{1,0:T(8,128)(2,1)S(1)}, bf16[512,512]{1,0:T(8,128)(2,1)}, u32[]{:S(2)}) copy-start(bf16[512,512]{1,0:T(8,128)(2,1)} %param.7) | copy-start | bytes 1572868
  161.3 12.6 %copy-start.12 = (bf16[512,512]{1,0:T(8,128)(2,1)S(1)}, bf16[512,512]{1,0:T(8,128)(2,1)}, u32[]{:S(2)}) copy-start(bf16[512,512]{1,0:T(8,128)(2,1)} %param.8) | copy-start | bytes 1572868
  161.3 12.6 %copy-start.16 = (bf16[1,128,1024]{2,1,0:T(8,128)(2,1)S(1)}, bf16[1,128,1024]{2,1,0:T(8,128)(2,1)}, u32[]{:S(2)}) copy-start(bf16[1,128,1024]{2,1,0:T(8,128)(2,1)} %param.11) | copy-start | bytes 786436
  161.6 26.2 %copy-start.15 = (bf16[1,128,1024]{2,1,0:T(8,128)(2,1)S(1)}, bf16[1,128,1024]{2,1,0:T(8,128)(2,1)}, u32[]{:S(2)}) copy-start(bf16[1,128,1024]{2,1,0:T(8,128)(2,1)} %param.6) | copy-start | bytes 786436
  161.8 25.7 %collective-permute-start.9 = (bf16[2,512,128]{1,2,0:T(8,128)(2,1)S(1)}, bf16[2,512,128]{1,2,0:T(8,128)(2,1)}, u32[]{:S(2)}, u32[]{:S(2)}) collective-permute-start(bf16[2,512,128]{1,2,0:T(8,128)(2,1)S(1)} %pad_maximum_fusion.9), channel_id=1, source_target_pairs={{0,1},{1,0},{2,3},{3,2},{4,5},{5,4},{6,7},{7,6},{8,9},{9,8},{10,11... | collective-permute-start | bytes 786440 | tf_op jit(solution)/shard_map/ppermute | solution.py:11
  161.9 11.9 %collective-permute-start.3 = (bf16[512,128]{0,1:T(8,128)(2,1)S(1)}, bf16[512,128]{0,1:T(8,128)(2,1)S(1)}, u32[]{:S(2)}, u32[]{:S(2)}) collective-permute-start(bf16[512,128]{0,1:T(8,128)(2,1)S(1)} %slice_bitcast_fusion.2), channel_id=1, source_target_pairs={{0,1},{1,0},{2,3},{3,2},{4,5},{5,4},{6,7},{7,6},{8,9},{9,8},{10,11... | collective-permute-start | bytes 393224 | tf_op jit(solution)/shard_map/ppermute | solution.py:11
  173.8 13.7 %collective-permute-start.4 = (bf16[512,128]{0,1:T(8,128)(2,1)S(1)}, bf16[512,128]{0,1:T(8,128)(2,1)S(1)}, u32[]{:S(2)}, u32[]{:S(2)}) collective-permute-start(bf16[512,128]{0,1:T(8,128)(2,1)S(1)} %collective-permute-done.3), channel_id=1, source_target_pairs={{0,2},{1,3},{2,0},{3,1},{4,6},{5,7},{6,4},{7,5},{8,10},{9,11},{10,... | collective-permute-start | bytes 393224 | tf_op jit(solution)/shard_map/ppermute | solution.py:11
  187.5 16.7 %collective-permute-start.5 = (bf16[512,128]{0,1:T(8,128)(2,1)S(1)}, bf16[512,128]{0,1:T(8,128)(2,1)S(1)}, u32[]{:S(2)}, u32[]{:S(2)}) collective-permute-start(bf16[512,128]{0,1:T(8,128)(2,1)S(1)} %collective-permute-done.4), channel_id=1, source_target_pairs={{0,4},{1,5},{2,6},{3,7},{4,0},{5,1},{6,2},{7,3},{8,12},{9,13},{10,... | collective-permute-start | bytes 393224 | tf_op jit(solution)/shard_map/ppermute | solution.py:11
  187.5 17.5 %collective-permute-start.10 = (bf16[2,512,128]{1,2,0:T(8,128)(2,1)}, bf16[2,512,128]{1,2,0:T(8,128)(2,1)S(1)}, u32[]{:S(2)}, u32[]{:S(2)}) collective-permute-start(bf16[2,512,128]{1,2,0:T(8,128)(2,1)} %collective-permute-done.9), channel_id=1, source_target_pairs={{0,2},{1,3},{2,0},{3,1},{4,6},{5,7},{6,4},{7,5},{8,10},{9,11},{10,... | collective-permute-start | bytes 786440 | tf_op jit(solution)/shard_map/ppermute | solution.py:11
  205.0 9.8 %collective-permute-start.11 = (bf16[2,512,128]{1,2,0:T(8,128)(2,1)S(1)}, bf16[2,512,128]{1,2,0:T(8,128)(2,1)S(1)}, u32[]{:S(2)}, u32[]{:S(2)}) collective-permute-start(bf16[2,512,128]{1,2,0:T(8,128)(2,1)S(1)} %collective-permute-done.10), channel_id=1, source_target_pairs={{0,4},{1,5},{2,6},{3,7},{4,0},{5,1},{6,2},{7,3},{8,12},{9,13},{10,... | collective-permute-start | bytes 786440 | tf_op jit(solution)/shard_map/ppermute | solution.py:11
  279.5 3.5 %copy-start.30 = (bf16[64,1024]{0,1:T(8,128)(2,1)S(1)}, bf16[64,1024]{0,1:T(8,128)(2,1)}, u32[]{:S(2)}) copy-start(bf16[64,1024]{0,1:T(8,128)(2,1)} %get-tuple-element.31) | copy-start | bytes 393220
Sparse Core Ops, SparseCore 0:
  157.9 85.8 reduce-scatter.3
  246.3 33.2 all-reduce.3
where the time goes:
time: 292 us; the launch traced here: 291 us
  waiting for transfers between devices  134 us (46%)
  local copies, waits for them, and re-layouts  52.8 us (18%)
  starting transfers between devices  35.6 us (12%)
  matrix products  31.2 us (11%)
  other arithmetic  22.3 us (8%)
  between operations  14.8 us (5%)
    ppermute x12, waiting for transfers between devices, swapped(): lax.ppermute(x, axis, [(i, i ^ 1 << stride) for i in range(lax.axis_size(...  57.8 us
    psum x1, waiting for transfers between devices, body(): lax.psum(share.astype(jnp.bfloat16), 'batch').astype(jnp.float32)  33 us
    unnamed x3, waiting for transfers between devices  27.5 us
    unnamed x76, local copies, waits for them, and re-layouts  16.4 us
    ppermute x12, starting transfers between devices, swapped(): lax.ppermute(x, axis, [(i, i ^ 1 << stride) for i in range(lax.axis_size(...  16.2 us
    all_to_all x2, starting transfers between devices, to_tokens(): lax.all_to_all(stacked, 'seq', split_axis=2, concat_axis=1, tiled=True)  9.78 us
    all_to_all x2, starting transfers between devices, to_channels(): lax.all_to_all(stacked, 'seq', split_axis=1, concat_axis=2, tiled=True)  9.47 us
    all_to_all x2, waiting for transfers between devices, to_tokens(): lax.all_to_all(stacked, 'seq', split_axis=2, concat_axis=1, tiled=True)  9.38 us
  transfers between devices with their start and end apart: 18, of which 14 were waited for; matrix products, arithmetic and copies ran while one was open for 10% of the time, Pallas kernels for 0%

commit v1 on v0

--- a/solution.py
+++ b/solution.py
@@ -5,6 +5,7 @@
 from jax.sharding import PartitionSpec as P
 
 precise = lax.Precision.HIGH
+open_inputs = lambda vector: jnp.sum(lax.all_gather(vector, "batch"), axis=0)
 
 
 def swapped(x, axis, stride):
@@ -176,7 +177,7 @@
         tiled=True,
     )
     share, filter_total = (
-        lax.psum(share.astype(jnp.bfloat16), "batch").astype(jnp.float32),
+        open_inputs(share.astype(jnp.bfloat16)).astype(jnp.float32),
         lax.psum(filter_part.astype(jnp.bfloat16), "batch").astype(jnp.float32),
     )
     return (

time: 292 us -> 255 us (0.87)
  waiting for transfers between devices: 134 us -> 84.3 us
  blocking collectives: 0 us -> 8.63 us
  starting transfers between devices: 35.6 us -> 41.1 us
    unnamed x3 -> x2, waiting for transfers between devices: 27.5 us -> 0.03 us
    psum x1, waiting for transfers between devices: 33 us -> 17.4 us  [body(): lax.psum(filter_part.astype(jnp.bfloat16), 'batch').astype(jnp.float32)]
    ppermute x12, waiting for transfers between devices: 57.8 us -> 46.3 us  [swapped(): lax.ppermute(x, axis, [(i, i ^ 1 << stride) for i in range(lax.axis_size(...]
    all_gather x0 -> x1, blocking collectives: none -> 8.63 us  [lax.all_gather(vector, 'batch')]
    reduce_scatter x0 -> x1, waiting for transfers between devices: none -> 7.63 us  [body(): lax.psum_scatter(jnp.concatenate([term_query, term_value, term_out], axis...]
    ppermute x12, starting transfers between devices: 16.2 us -> 21.8 us  [swapped(): lax.ppermute(x, axis, [(i, i ^ 1 << stride) for i in range(lax.axis_size(...]
    unnamed x76 -> x68, local copies, waits for them, and re-layouts: 16.4 us -> 13.5 us
  transfers between devices with their start and end apart: 18 -> 18, of which waited for: 14 -> 15; matrix products, arithmetic and copies ran while one was open for 10% -> 17% of each run, Pallas kernels for 0% -> 0%
where the time goes in v1:
time: 255 us; the launch traced here: 253 us
  waiting for transfers between devices  84.3 us (33%)
  local copies, waits for them, and re-layouts  50.4 us (20%)
  starting transfers between devices  41.1 us (16%)
  matrix products  29.3 us (11%)
  other arithmetic  23.4 us (9%)
  between operations  16.2 us (6%)
  blocking collectives  8.63 us (3%)
    ppermute x12, waiting for transfers between devices, swapped(): lax.ppermute(x, axis, [(i, i ^ 1 << stride) for i in range(lax.axis_size(...  46.3 us
    ppermute x12, starting transfers between devices, swapped(): lax.ppermute(x, axis, [(i, i ^ 1 << stride) for i in range(lax.axis_size(...  21.8 us
    psum x1, waiting for transfers between devices, body(): lax.psum(filter_part.astype(jnp.bfloat16), 'batch').astype(jnp.float32)  17.4 us
    unnamed x68, local copies, waits for them, and re-layouts  13.5 us
    all_to_all x2, starting transfers between devices, to_tokens(): lax.all_to_all(stacked, 'seq', split_axis=2, concat_axis=1, tiled=True)  9.76 us
    all_to_all x2, starting transfers between devices, to_channels(): lax.all_to_all(stacked, 'seq', split_axis=1, concat_axis=2, tiled=True)  9.46 us
    another operation x3, local copies, waits for them, and re-layouts, forward_spectrum(): jnp.stack([section[0] * cos_twist + section[1] * sin_twist, section[1] *...  9.36 us
    all_gather x1, blocking collectives, lax.all_gather(vector, 'batch')  8.63 us
  transfers between devices with their start and end apart: 18, of which 15 were waited for; matrix products, arithmetic and copies ran while one was open for 17% of the time, Pallas kernels for 0%

profile of v1, /device:TPU:0, one launch (start us, length us, event | category | flops | bytes accessed | tf_op | source)
XLA Modules:
  0.0 253.3 jit_solution(7137198861297130004)
XLA Ops:
  8.0 1.0 slice_bitcast_fusion.6
  9.1 3.0 %collective-permute-start = (bf16[128,512]{1,0:T(8,128)(2,1)S(1)}, bf16[128,512]{1,0:T(8,128)(2,1)S(1)}, u32[]{:S(2)}, u32[]{:S(2)}) collective-permute-start(bf16[128,512]{1,0:T(8,128)(2,1)S(1)} %get-tuple-element.53), channel_id=1, source_target_pairs={{0,1},{1,0},{2,3},{3,2},{4,5},{5,4},{6,7},{7,6},{8,9},{9,8},{10,11... | collective-permute-start | bytes 393224 | tf_op jit(solution)/shard_map/ppermute | solution.py:12
  13.2 2.8 %collective-permute-done = bf16[128,512]{1,0:T(8,128)(2,1)S(1)} collective-permute-done((bf16[128,512]{1,0:T(8,128)(2,1)S(1)}, bf16[128,512]{1,0:T(8,128)(2,1)S(1)}, u32[]{:S(2)}, u32[]{:S(2)}) %collective-permute-start) | collective-permute-done | bytes 131104 | tf_op jit(solution)/shard_map/ppermute | solution.py:12
  16.0 2.0 collective-permute-start.1
  18.4 1.8 collective-permute-start.7
  20.2 1.4 collective-permute-done.1
  21.6 3.2 %collective-permute-start.2 = (bf16[128,512]{1,0:T(8,128)(2,1)S(1)}, bf16[128,512]{1,0:T(8,128)(2,1)S(1)}, u32[]{:S(2)}, u32[]{:S(2)}) collective-permute-start(bf16[128,512]{1,0:T(8,128)(2,1)S(1)} %collective-permute-done.1), channel_id=1, source_target_pairs={{0,4},{1,5},{2,6},{3,7},{4,0},{5,1},{6,2},{7,3},{8,12},{9,13},{10,... | collective-permute-start | bytes 393224 | tf_op jit(solution)/shard_map/ppermute | solution.py:12
  25.2 2.4 collective-permute-start.8
  27.6 6.2 %collective-permute-done.2 = bf16[128,512]{1,0:T(8,128)(2,1)S(1)} collective-permute-done((bf16[128,512]{1,0:T(8,128)(2,1)S(1)}, bf16[128,512]{1,0:T(8,128)(2,1)S(1)}, u32[]{:S(2)}, u32[]{:S(2)}) %collective-permute-start.2) | collective-permute-done | bytes 131104 | tf_op jit(solution)/shard_map/ppermute | solution.py:12
  34.2 1.3 fusion.63
  36.1 1.1 multiply_convert_fusion
  38.1 5.2 %all-to-all-start.2 = ((bf16[2,512,128]{2,0,1:T(2,128)(2,1)}), bf16[2,512,128]{2,0,1:T(2,128)(2,1)S(1)}, u32[]{:S(2)}, u32[]{:S(2)}) async-start(bf16[2,512,128]{2,0,1:T(2,128)(2,1)} %copy.133), calls=%async_computation.2 | async-start | bytes 524288 | tf_op jit(solution)/shard_map/all_to_all | solution.py:97
  45.3 6.3 %all-to-all-done.2 = bf16[2,512,128]{2,0,1:T(2,128)(2,1)S(1)} async-done(((bf16[2,512,128]{2,0,1:T(2,128)(2,1)}), bf16[2,512,128]{2,0,1:T(2,128)(2,1)S(1)}, u32[]{:S(2)}, u32[]{:S(2)}) %all-to-all-start.2) | async-done | bytes 262176 | tf_op jit(solution)/shard_map/all_to_all | solution.py:97
  51.6 4.2 %all-to-all-start = ((bf16[2,512,128]{2,0,1:T(2,128)(2,1)}), bf16[2,512,128]{2,0,1:T(2,128)(2,1)}, u32[]{:S(2)}, u32[]{:S(2)}) async-start(bf16[2,512,128]{2,0,1:T(2,128)(2,1)} %copy.115), calls=%async_computation | async-start | bytes 524288 | tf_op jit(solution)/shard_map/all_to_all | solution.py:97
  57.5 1.5 convolution_bitcast_fusion
  59.7 1.9 copy.135
  61.7 3.2 %convolution_bitcast_fusion.1 = f32[2,64,64,32]{1,2,3,0:T(8,128)} fusion(bf16[2,64,32,32]{1,3,2,0:T(8,128)(2,1)} %bitcast.318, f32[1,2,64,64]{3,2,1,0:T(8,128)S(1)} %get-tuple-element.58, f32[1,2,64,64]{3,2,1,0:T(8,128)S(1)} %get-tuple-element.69), kind=kOutput, calls=%fused_computation.41 | convolution fusion | flops 100671488 | bytes 1376256 | tf_op jit(solution)/shard_map/brnm,abnk->arkm/dot_general | solution.py:50
  64.8 1.7 copy.116
  66.5 1.9 copy.117
  68.5 1.9 convolution_bitcast_fusion.2
  70.5 2.6 %multiply_add_fusion.4 = (f32[1,64,64,32]{1,2,3,0:T(8,128)}, f32[1,64,64,32]{1,2,3,0:T(8,128)}, f32[1,64,64,32]{1,2,3,0:T(8,128)S(1)}, f32[1,64,64,32]{1,2,3,0:T...) fusion(f32[2,64,64,32]{1,2,3,0:T(8,128)S(1)} %copy-done.4, f32[64,32]{0,1:T(8,128)S(1)} %get-tuple-element.81, ...), kind=kLoop, calls=%fused_computation.85 | loop fusion | flops 2359296 | bytes 6307840 | tf_op jit(solution)/shard_map/add | solution.py:53
  73.3 2.8 %copy.122 = f32[2,64,64,32]{2,3,0,1:T(8,128)} copy(f32[2,64,64,32]{1,2,3,0:T(8,128)S(1)} %pad_maximum_fusion.1) | data formatting | bytes 2097152 | tf_op jit(solution)/shard_map/stack | solution.py:51
  76.0 1.7 pad_maximum_fusion.3
  77.8 2.8 %copy.137 = f32[2,64,64,32]{2,3,0,1:T(8,128)} copy(f32[2,64,64,32]{1,2,3,0:T(8,128)S(1)} %pad_maximum_fusion.3) | data formatting | bytes 2097152 | tf_op jit(solution)/shard_map/stack | solution.py:51
  80.5 2.8 %fusion.28 = f32[2,64,64,32]{2,3,1,0:T(8,128)S(1)} fusion(f32[2,64,64,32]{2,3,0,1:T(8,128)} %copy.122, f32[1,2,32,32]{2,3,1,0:T(8,128)S(1)} %copy-done.22, f32[1,2,32,32]{2,3,1,0:T(8,128)S(1)} %copy-done.23), kind=kOutput, calls=%fused_computation.35 | convolution fusion | flops 100667392 | bytes 2113536 | tf_op jit(solution)/shard_map/brkm,abmj->arkj/dot_general | solution.py:57
  83.3 1.1 fusion.34
  85.8 2.4 fusion.37
  88.2 3.3 %copy.139 = f32[2,32,64,64]{2,3,1,0:T(8,128)} copy(f32[2,32,64,64]{3,1,2,0:T(8,128)} %fusion.37) | data formatting | bytes 2097152 | tf_op jit(solution)/shard_map/brkj,abjm->arkm/dot_general | solution.py:64
  91.6 3.2 %pad_maximum_fusion = f32[2,64,64,32]{1,2,3,0:T(8,128)} fusion(f32[1,64,64,32]{1,2,3,0:T(8,128)} %get-tuple-element.67, f32[1,64,64,32]{1,2,3,0:T(8,128)} %get-tuple-element.68), kind=kLoop, calls=%fused_computation.1 | loop fusion | flops 262144 | bytes 2097152 | tf_op jit(solution)/shard_map/stack | solution.py:51
  94.7 3.8 %copy.119 = f32[2,64,64,32]{2,3,0,1:T(8,128)} copy(f32[2,64,64,32]{1,2,3,0:T(8,128)} %pad_maximum_fusion) | data formatting | bytes 2097152 | tf_op jit(solution)/shard_map/stack | solution.py:51
  98.6 2.8 %fusion.25 = f32[2,64,64,32]{2,3,1,0:T(8,128)S(1)} fusion(f32[2,64,64,32]{2,3,0,1:T(8,128)} %copy.119, f32[1,2,32,32]{2,3,1,0:T(8,128)S(1)} %copy-done.22, f32[1,2,32,32]{2,3,1,0:T(8,128)S(1)} %copy-done.23), kind=kOutput, calls=%fused_computation.34 | convolution fusion | flops 100667392 | bytes 2113536 | tf_op jit(solution)/shard_map/brkm,abmj->arkj/dot_general | solution.py:57
  101.4 2.2 multiply_add_fusion.1
  104.6 2.2 copy.124
  106.8 2.6 %fusion.40 = f32[2,32,64,64]{3,1,2,0:T(8,128)S(1)} fusion(f32[1,2,32,32]{2,3,1,0:T(8,128)S(1)} %copy-done.21, f32[1,2,32,32]{2,3,1,0:T(8,128)S(1)} %copy-done.20, f32[1,64,64,32]{2,3,1,0:T(8,128)} %get-tuple-element.25, f32[1,64,64,32]{2,3,1,0:T(8,128)} %get-tuple-element.24), kind=kOutput, calls=%fused_computation.39 | convolution fusion | flops 100929536 | bytes 2113536 | tf_op jit(solution)/shard_map/brkj,abjm->arkm/dot_general | solution.py:64
  109.4 2.3 copy.154
  111.6 4.4 %multiply_subtract_fusion = (f32[1,64,64,32]{1,2,3,0:T(8,128)S(1)}, f32[1,64,64,32]{1,2,3,0:T(8,128)S(1)}, f32[1,64,64,32]{1,2,3,0:T(8,128)}, f32[1,64,64,32]{1,...) fusion(f32[2,64,64,32]{1,2,3,0:T(8,128)} %bitcast.300, f32[64,32]{0,1:T(8,128)S(1)} %get-tuple-element.81, ...), kind=kLoop, calls=%fused_computation.77 | loop fusion | flops 2359296 | bytes 6307840 | tf_op jit(solution)/shard_map/sub | solution.py:66
  117.0 1.4 copy.230
  118.4 2.1 reshape.297
  120.5 5.7 %all-to-all-start.3 = ((bf16[8,2,8192]{2,1,0:T(2,128)(2,1)}), bf16[8,2,8192]{2,1,0:T(2,128)(2,1)}, u32[]{:S(2)}, u32[]{:S(2)}) async-start(bf16[8,2,8192]{2,1,0:T(2,128)(2,1)} %reshape.297), calls=%async_computation.3 | async-start | bytes 524288 | tf_op jit(solution)/shard_map/all_to_all | solution.py:101
  126.2 2.2 fusion.52
  128.7 1.4 copy.231
  130.1 2.1 reshape.295
  132.2 2.4 all-to-all-done.3
  134.6 4.0 %all-to-all-start.1 = ((bf16[8,2,8192]{2,1,0:T(2,128)(2,1)}), bf16[8,2,8192]{2,1,0:T(2,128)(2,1)}, u32[]{:S(2)}, u32[]{:S(2)}) async-start(bf16[8,2,8192]{2,1,0:T(2,128)(2,1)} %reshape.295), calls=%async_computation.1 | async-start | bytes 524288 | tf_op jit(solution)/shard_map/all_to_all | solution.py:101
  140.2 1.3 reshape.298
  142.6 4.3 %all-to-all-done.1 = bf16[8,2,8192]{2,1,0:T(2,128)(2,1)} async-done(((bf16[8,2,8192]{2,1,0:T(2,128)(2,1)}), bf16[8,2,8192]{2,1,0:T(2,128)(2,1)}, u32[]{:S(2)}, u32[]{:S(2)}) %all-to-all-start.1) | async-done | bytes 262176 | tf_op jit(solution)/shard_map/all_to_all | solution.py:101
  146.9 1.3 reshape.296
  149.8 1.4 multiply_convert_fusion.1
  151.3 1.4 convolution_bitcast_fusion.4
  153.0 2.1 maximum_multiply_fusion
  155.1 3.5 %copy.195 = f32[512,1536]{1,0:T(8,128)} copy(f32[512,1536]{0,1:T(8,128)} %maximum_multiply_fusion) | data formatting | bytes 6291456
  158.6 17.4 %all-reduce.3.cloned.1.call-done = bf16[64,1024]{0,1:T(8,128)(2,1)} async-done(((bf16[64,1024]{0,1:T(8,128)(2,1)}), bf16[64,1024]{0,1:T(8,128)(2,1)}) %all-reduce.3.cloned.1.call-update) | async-done | bytes 131088 | tf_op jit(solution)/shard_map/psum | solution.py:181
  176.0 1.8 copy.158
  178.3 1.5 collective-permute-start.9
  180.8 11.3 %collective-permute-done.3 = bf16[512,128]{0,1:T(8,128)(2,1)S(1)} collective-permute-done((bf16[512,128]{0,1:T(8,128)(2,1)S(1)}, bf16[512,128]{0,1:T(8,128)(2,1)S(1)}, u32[]{:S(2)}, u32[]{:S(2)}) %collective-permute-start.3) | collective-permute-done | bytes 131104 | tf_op jit(solution)/shard_map/ppermute | solution.py:12
  192.1 2.1 collective-permute-start.4
  194.5 2.6 %collective-permute-done.4 = bf16[512,128]{0,1:T(8,128)(2,1)S(1)} collective-permute-done((bf16[512,128]{0,1:T(8,128)(2,1)S(1)}, bf16[512,128]{0,1:T(8,128)(2,1)S(1)}, u32[]{:S(2)}, u32[]{:S(2)}) %collective-permute-start.4) | collective-permute-done | bytes 131104 | tf_op jit(solution)/shard_map/ppermute | solution.py:12
  197.1 3.0 %collective-permute-start.5 = (bf16[512,128]{0,1:T(8,128)(2,1)S(1)}, bf16[512,128]{0,1:T(8,128)(2,1)S(1)}, u32[]{:S(2)}, u32[]{:S(2)}) collective-permute-start(bf16[512,128]{0,1:T(8,128)(2,1)S(1)} %collective-permute-done.4), channel_id=1, source_target_pairs={{0,4},{1,5},{2,6},{3,7},{4,0},{5,1},{6,2},{7,3},{8,12},{9,13},{10,... | collective-permute-start | bytes 393224 | tf_op jit(solution)/shard_map/ppermute | solution.py:12
  201.3 2.9 %collective-permute-done.5 = bf16[512,128]{0,1:T(8,128)(2,1)S(1)} collective-permute-done((bf16[512,128]{0,1:T(8,128)(2,1)S(1)}, bf16[512,128]{0,1:T(8,128)(2,1)S(1)}, u32[]{:S(2)}, u32[]{:S(2)}) %collective-permute-start.5) | collective-permute-done | bytes 131104 | tf_op jit(solution)/shard_map/ppermute | solution.py:12
  205.0 3.3 %collective-permute-done.10 = bf16[2,512,128]{1,2,0:T(8,128)(2,1)S(1)} collective-permute-done((bf16[2,512,128]{1,2,0:T(8,128)(2,1)}, bf16[2,512,128]{1,2,0:T(8,128)(2,1)S(1)}, u32[]{:S(2)}, u32[]{:S(2)}) %collective-permute-start.10) | collective-permute-done | bytes 262176 | tf_op jit(solution)/shard_map/ppermute | solution.py:12
  208.3 1.1 collective-permute-start.11
  210.2 15.3 %collective-permute-done.11 = bf16[2,512,128]{1,2,0:T(8,128)(2,1)S(1)} collective-permute-done((bf16[2,512,128]{1,2,0:T(8,128)(2,1)S(1)}, bf16[2,512,128]{1,2,0:T(8,128)(2,1)S(1)}, u32[]{:S(2)}, u32[]{:S(2)}) %collective-permute-start.11) | collective-permute-done | bytes 262176 | tf_op jit(solution)/shard_map/ppermute | solution.py:12
  227.7 7.6 %reduce-scatter.4.cloned.1.call-done = f32[64,1536]{1,0:T(8,128)} async-done(((f32[512,1536]{1,0:T(8,128)}), f32[64,1536]{1,0:T(8,128)}) %reduce-scatter.4.cloned.1.call-update) | async-done | bytes 393232 | tf_op jit(solution)/shard_map/reduce_scatter | solution.py:173
  236.3 8.6 %all-gather = bf16[256,1536]{1,0:T(8,128)(2,1)S(1)} all-gather(bf16[64,1536]{1,0:T(8,128)(2,1)S(1)} %convert_element_type.266), channel_id=2, replica_groups=mesh['batch'=4,'seq'=8] {'batch'}, dimensions={0}, use_global_device_ids=true | all-gather | bytes 983040 | tf_op jit(solution)/shard_map/all_gather | solution.py:8
  (131 shorter events, 24.8 us)
Async XLA Ops:
  8.0 28.1 %copy-start = (bf16[512,512]{1,0:T(8,128)(2,1)S(1)}, bf16[512,512]{1,0:T(8,128)(2,1)}, u32[]{:S(2)}) copy-start(bf16[512,512]{1,0:T(8,128)(2,1)} %param.9) | copy-start | bytes 1572868
  9.1 133.2 %copy-start.8 = (bf16[1,128,512]{2,1,0:T(8,128)(2,1)}, bf16[1,128,512]{2,1,0:T(8,128)(2,1)S(1)}, u32[]{:S(2)}) copy-start(bf16[1,128,512]{2,1,0:T(8,128)(2,1)S(1)} %get-tuple-element.52) | copy-start | bytes 393220
  9.1 6.9 %collective-permute-start = (bf16[128,512]{1,0:T(8,128)(2,1)S(1)}, bf16[128,512]{1,0:T(8,128)(2,1)S(1)}, u32[]{:S(2)}, u32[]{:S(2)}) collective-permute-start(bf16[128,512]{1,0:T(8,128)(2,1)S(1)} %get-tuple-element.53), channel_id=1, source_target_pairs={{0,1},{1,0},{2,3},{3,2},{4,5},{5,4},{6,7},{7,6},{8,9},{9,8},{10,11... | collective-permute-start | bytes 393224 | tf_op jit(solution)/shard_map/ppermute | solution.py:12
  13.1 25.0 %copy-start.13 = (bf16[1,128,512]{2,1,0:T(8,128)(2,1)}, bf16[1,128,512]{2,1,0:T(8,128)(2,1)S(1)}, u32[]{:S(2)}) copy-start(bf16[1,128,512]{2,1,0:T(8,128)(2,1)S(1)} %get-tuple-element.50) | copy-start | bytes 393220
  13.1 5.3 %collective-permute-start.6 = (bf16[128,512]{1,0:T(8,128)(2,1)S(1)}, bf16[128,512]{1,0:T(8,128)(2,1)S(1)}, u32[]{:S(2)}, u32[]{:S(2)}) collective-permute-start(bf16[128,512]{1,0:T(8,128)(2,1)S(1)} %get-tuple-element.51), channel_id=1, source_target_pairs={{0,1},{1,0},{2,3},{3,2},{4,5},{5,4},{6,7},{7,6},{8,9},{9,8},{10,11... | collective-permute-start | bytes 393224 | tf_op jit(solution)/shard_map/ppermute | solution.py:12
  16.0 5.6 %collective-permute-start.1 = (bf16[128,512]{1,0:T(8,128)(2,1)S(1)}, bf16[128,512]{1,0:T(8,128)(2,1)S(1)}, u32[]{:S(2)}, u32[]{:S(2)}) collective-permute-start(bf16[128,512]{1,0:T(8,128)(2,1)S(1)} %collective-permute-done), channel_id=1, source_target_pairs={{0,2},{1,3},{2,0},{3,1},{4,6},{5,7},{6,4},{7,5},{8,10},{9,11},{10,... | collective-permute-start | bytes 393224 | tf_op jit(solution)/shard_map/ppermute | solution.py:12
  18.1 38.7 %copy-start.24 = (f32[1,64,64]{2,1,0:T(8,128)}, f32[1,64,64]{2,1,0:T(8,128)S(1)}, u32[]{:S(2)}) copy-start(f32[1,64,64]{2,1,0:T(8,128)S(1)} %fusion.120) | copy-start | bytes 49156
  18.4 6.8 %collective-permute-start.7 = (bf16[128,512]{1,0:T(8,128)(2,1)S(1)}, bf16[128,512]{1,0:T(8,128)(2,1)S(1)}, u32[]{:S(2)}, u32[]{:S(2)}) collective-permute-start(bf16[128,512]{1,0:T(8,128)(2,1)S(1)} %collective-permute-done.6), channel_id=1, source_target_pairs={{0,2},{1,3},{2,0},{3,1},{4,6},{5,7},{6,4},{7,5},{8,10},{9,11},{10,... | collective-permute-start | bytes 393224 | tf_op jit(solution)/shard_map/ppermute | solution.py:12
  21.6 12.2 %collective-permute-start.2 = (bf16[128,512]{1,0:T(8,128)(2,1)S(1)}, bf16[128,512]{1,0:T(8,128)(2,1)S(1)}, u32[]{:S(2)}, u32[]{:S(2)}) collective-permute-start(bf16[128,512]{1,0:T(8,128)(2,1)S(1)} %collective-permute-done.1), channel_id=1, source_target_pairs={{0,4},{1,5},{2,6},{3,7},{4,0},{5,1},{6,2},{7,3},{8,12},{9,13},{10,... | collective-permute-start | bytes 393224 | tf_op jit(solution)/shard_map/ppermute | solution.py:12
  25.0 31.8 %copy-start.26 = (f32[1,64,64]{2,1,0:T(8,128)}, f32[1,64,64]{2,1,0:T(8,128)S(1)}, u32[]{:S(2)}) copy-start(f32[1,64,64]{2,1,0:T(8,128)S(1)} %get-tuple-element.79) | copy-start | bytes 49156
  25.2 10.5 %collective-permute-start.8 = (bf16[128,512]{1,0:T(8,128)(2,1)S(1)}, bf16[128,512]{1,0:T(8,128)(2,1)S(1)}, u32[]{:S(2)}, u32[]{:S(2)}) collective-permute-start(bf16[128,512]{1,0:T(8,128)(2,1)S(1)} %collective-permute-done.7), channel_id=1, source_target_pairs={{0,4},{1,5},{2,6},{3,7},{4,0},{5,1},{6,2},{7,3},{8,12},{9,13},{10,... | collective-permute-start | bytes 393224 | tf_op jit(solution)/shard_map/ppermute | solution.py:12
  35.6 8.5 %copy-start.10 = (bf16[512,512]{1,0:T(8,128)(2,1)S(1)}, bf16[512,512]{1,0:T(8,128)(2,1)}, u32[]{:S(2)}) copy-start(bf16[512,512]{1,0:T(8,128)(2,1)} %param.8) | copy-start | bytes 1572868
  36.1 8.3 %copy-start.12 = (bf16[128,512]{1,0:T(8,128)(2,1)}, bf16[128,512]{1,0:T(8,128)(2,1)S(1)}, u32[]{:S(2)}) copy-start(bf16[128,512]{1,0:T(8,128)(2,1)S(1)} %rev.24) | copy-start | bytes 393220
  37.3 19.3 %copy-start.28 = (f32[64,1024]{1,0:T(8,128)S(1)}, f32[64,1024]{1,0:T(8,128)}, u32[]{:S(2)}) copy-start(f32[64,1024]{1,0:T(8,128)} %param.10) | copy-start | bytes 786436
  38.1 13.5 %all-to-all-start.2 = ((bf16[2,512,128]{2,0,1:T(2,128)(2,1)}), bf16[2,512,128]{2,0,1:T(2,128)(2,1)S(1)}, u32[]{:S(2)}, u32[]{:S(2)}) async-start(bf16[2,512,128]{2,0,1:T(2,128)(2,1)} %copy.133), calls=%async_computation.2 | async-start | bytes 524288 | tf_op jit(solution)/shard_map/all_to_all | solution.py:97
  51.6 5.9 %copy-start.16 = (bf16[2,512,128]{2,0,1:T(2,128)(2,1)}, bf16[2,512,128]{2,0,1:T(2,128)(2,1)S(1)}, u32[]{:S(2)}) copy-start(bf16[2,512,128]{2,0,1:T(2,128)(2,1)S(1)} %all-to-all-done.2) | copy-start | bytes 786436
  51.6 13.2 %all-to-all-start = ((bf16[2,512,128]{2,0,1:T(2,128)(2,1)}), bf16[2,512,128]{2,0,1:T(2,128)(2,1)}, u32[]{:S(2)}, u32[]{:S(2)}) async-start(bf16[2,512,128]{2,0,1:T(2,128)(2,1)} %copy.115), calls=%async_computation | async-start | bytes 524288 | tf_op jit(solution)/shard_map/all_to_all | solution.py:97
  57.5 1.5 copy-start.17
  68.5 2.0 copy-start.4
  68.5 2.0 copy-start.29
  77.7 2.8 %copy-start.22 = (f32[1,2,32,32]{2,3,1,0:T(8,128)S(1)}, f32[1,2,32,32]{2,3,1,0:T(8,128)}, u32[]{:S(2)}) copy-start(f32[1,2,32,32]{2,3,1,0:T(8,128)} %get-tuple-element.72) | copy-start | bytes 24580
  77.8 2.8 %copy-start.23 = (f32[1,2,32,32]{2,3,1,0:T(8,128)S(1)}, f32[1,2,32,32]{2,3,1,0:T(8,128)}, u32[]{:S(2)}) copy-start(f32[1,2,32,32]{2,3,1,0:T(8,128)} %get-tuple-element.75) | copy-start | bytes 24580
  80.5 2.8 %copy-start.3 = (f32[2,64,64,32]{2,3,0,1:T(8,128)S(1)}, f32[2,64,64,32]{2,3,0,1:T(8,128)}, u32[]{:S(2)}) copy-start(f32[2,64,64,32]{2,3,0,1:T(8,128)} %copy.137) | copy-start | bytes 3145732
  84.4 1.4 copy-start.1
  84.4 1.4 copy-start.20
  84.4 1.4 copy-start.21
  98.6 2.8 %copy-start.2 = (f32[2,64,64,32]{2,3,1,0:T(8,128)S(1)}, f32[2,64,64,32]{2,3,1,0:T(8,128)}, u32[]{:S(2)}) copy-start(f32[2,64,64,32]{2,3,1,0:T(8,128)} %copy-done.1) | copy-start | bytes 3145732
  111.6 4.4 %copy-start.18 = (f32[1,2,64,64]{3,2,1,0:T(8,128)S(1)}, f32[1,2,64,64]{3,2,1,0:T(8,128)}, u32[]{:S(2)}) copy-start(f32[1,2,64,64]{3,2,1,0:T(8,128)} %get-tuple-element.57) | copy-start | bytes 98308
  111.6 4.4 %copy-start.19 = (f32[1,2,64,64]{3,2,1,0:T(8,128)S(1)}, f32[1,2,64,64]{3,2,1,0:T(8,128)}, u32[]{:S(2)}) copy-start(f32[1,2,64,64]{3,2,1,0:T(8,128)} %get-tuple-element.70) | copy-start | bytes 98308
  120.5 14.1 %all-to-all-start.3 = ((bf16[8,2,8192]{2,1,0:T(2,128)(2,1)}), bf16[8,2,8192]{2,1,0:T(2,128)(2,1)}, u32[]{:S(2)}, u32[]{:S(2)}) async-start(bf16[8,2,8192]{2,1,0:T(2,128)(2,1)} %reshape.297), calls=%async_computation.3 | async-start | bytes 524288 | tf_op jit(solution)/shard_map/all_to_all | solution.py:101
  128.5 10.2 %copy-start.25 = (f32[1,64,64]{2,1,0:T(8,128)S(1)}, f32[1,64,64]{2,1,0:T(8,128)}, u32[]{:S(2)}) copy-start(f32[1,64,64]{2,1,0:T(8,128)} %copy-done.24) | copy-start | bytes 49156
  128.5 10.2 %copy-start.27 = (f32[1,64,64]{2,1,0:T(8,128)S(1)}, f32[1,64,64]{2,1,0:T(8,128)}, u32[]{:S(2)}) copy-start(f32[1,64,64]{2,1,0:T(8,128)} %copy-done.26) | copy-start | bytes 49156
  134.6 12.3 %all-to-all-start.1 = ((bf16[8,2,8192]{2,1,0:T(2,128)(2,1)}), bf16[8,2,8192]{2,1,0:T(2,128)(2,1)}, u32[]{:S(2)}, u32[]{:S(2)}) async-start(bf16[8,2,8192]{2,1,0:T(2,128)(2,1)} %reshape.295), calls=%async_computation.1 | async-start | bytes 524288 | tf_op jit(solution)/shard_map/all_to_all | solution.py:101
  138.6 37.4 %all-reduce.3.cloned.1.call-start = ((), (), s32[]{:S(2)}) async-start(), calls=%async_computation.5 | async-start | bytes 524288 | tf_op jit(solution)/shard_map/psum | solution.py:181
  140.2 95.1 %reduce-scatter.4.cloned.1.call-start = ((), (), s32[]{:S(2)}) async-start(), calls=%async_computation.6 | async-start | bytes 3538944 | tf_op jit(solution)/shard_map/reduce_scatter | solution.py:173
  149.8 2.9 %copy-start.9 = (bf16[1,128,512]{2,1,0:T(8,128)(2,1)S(1)}, bf16[1,128,512]{2,1,0:T(8,128)(2,1)}, u32[]{:S(2)}) copy-start(bf16[1,128,512]{2,1,0:T(8,128)(2,1)} %copy-done.8) | copy-start | bytes 393220
  151.2 1.4 copy-start.6
  158.6 19.5 %copy-start.7 = (bf16[2,512,128]{1,2,0:T(8,128)(2,1)S(1)}, bf16[2,512,128]{1,2,0:T(8,128)(2,1)}, u32[]{:S(2)}) copy-start(bf16[2,512,128]{1,2,0:T(8,128)(2,1)} %copy-done.6) | copy-start | bytes 786436
  158.6 21.9 %copy-start.5 = (bf16[512,512]{1,0:T(8,128)(2,1)S(1)}, bf16[512,512]{1,0:T(8,128)(2,1)}, u32[]{:S(2)}) copy-start(bf16[512,512]{1,0:T(8,128)(2,1)} %param.7) | copy-start | bytes 1572868
  177.8 16.4 %copy-start.11 = (bf16[512,512]{1,0:T(8,128)(2,1)S(1)}, bf16[512,512]{1,0:T(8,128)(2,1)}, u32[]{:S(2)}) copy-start(bf16[512,512]{1,0:T(8,128)(2,1)} %param.8) | copy-start | bytes 1572868
  177.8 16.4 %copy-start.15 = (bf16[1,128,1024]{2,1,0:T(8,128)(2,1)S(1)}, bf16[1,128,1024]{2,1,0:T(8,128)(2,1)}, u32[]{:S(2)}) copy-start(bf16[1,128,1024]{2,1,0:T(8,128)(2,1)} %param.11) | copy-start | bytes 786436
  178.1 23.0 %copy-start.14 = (bf16[1,128,1024]{2,1,0:T(8,128)(2,1)S(1)}, bf16[1,128,1024]{2,1,0:T(8,128)(2,1)}, u32[]{:S(2)}) copy-start(bf16[1,128,1024]{2,1,0:T(8,128)(2,1)} %param.6) | copy-start | bytes 786436
  178.3 21.8 %collective-permute-start.9 = (bf16[2,512,128]{1,2,0:T(8,128)(2,1)S(1)}, bf16[2,512,128]{1,2,0:T(8,128)(2,1)}, u32[]{:S(2)}, u32[]{:S(2)}) collective-permute-start(bf16[2,512,128]{1,2,0:T(8,128)(2,1)S(1)} %pad_maximum_fusion.9), channel_id=1, source_target_pairs={{0,1},{1,0},{2,3},{3,2},{4,5},{5,4},{6,7},{7,6},{8,9},{9,8},{10,11... | collective-permute-start | bytes 786440 | tf_op jit(solution)/shard_map/ppermute | solution.py:12
  179.9 12.2 %collective-permute-start.3 = (bf16[512,128]{0,1:T(8,128)(2,1)S(1)}, bf16[512,128]{0,1:T(8,128)(2,1)S(1)}, u32[]{:S(2)}, u32[]{:S(2)}) collective-permute-start(bf16[512,128]{0,1:T(8,128)(2,1)S(1)} %slice_bitcast_fusion.2), channel_id=1, source_target_pairs={{0,1},{1,0},{2,3},{3,2},{4,5},{5,4},{6,7},{7,6},{8,9},{9,8},{10,11... | collective-permute-start | bytes 393224 | tf_op jit(solution)/shard_map/ppermute | solution.py:12
  192.1 5.0 %collective-permute-start.4 = (bf16[512,128]{0,1:T(8,128)(2,1)S(1)}, bf16[512,128]{0,1:T(8,128)(2,1)S(1)}, u32[]{:S(2)}, u32[]{:S(2)}) collective-permute-start(bf16[512,128]{0,1:T(8,128)(2,1)S(1)} %collective-permute-done.3), channel_id=1, source_target_pairs={{0,2},{1,3},{2,0},{3,1},{4,6},{5,7},{6,4},{7,5},{8,10},{9,11},{10,... | collective-permute-start | bytes 393224 | tf_op jit(solution)/shard_map/ppermute | solution.py:12
  197.1 7.1 %collective-permute-start.5 = (bf16[512,128]{0,1:T(8,128)(2,1)S(1)}, bf16[512,128]{0,1:T(8,128)(2,1)S(1)}, u32[]{:S(2)}, u32[]{:S(2)}) collective-permute-start(bf16[512,128]{0,1:T(8,128)(2,1)S(1)} %collective-permute-done.4), channel_id=1, source_target_pairs={{0,4},{1,5},{2,6},{3,7},{4,0},{5,1},{6,2},{7,3},{8,12},{9,13},{10,... | collective-permute-start | bytes 393224 | tf_op jit(solution)/shard_map/ppermute | solution.py:12
  200.1 8.2 %collective-permute-start.10 = (bf16[2,512,128]{1,2,0:T(8,128)(2,1)}, bf16[2,512,128]{1,2,0:T(8,128)(2,1)S(1)}, u32[]{:S(2)}, u32[]{:S(2)}) collective-permute-start(bf16[2,512,128]{1,2,0:T(8,128)(2,1)} %collective-permute-done.9), channel_id=1, source_target_pairs={{0,2},{1,3},{2,0},{3,1},{4,6},{5,7},{6,4},{7,5},{8,10},{9,11},{10,... | collective-permute-start | bytes 786440 | tf_op jit(solution)/shard_map/ppermute | solution.py:12
  208.3 17.2 %collective-permute-start.11 = (bf16[2,512,128]{1,2,0:T(8,128)(2,1)S(1)}, bf16[2,512,128]{1,2,0:T(8,128)(2,1)S(1)}, u32[]{:S(2)}, u32[]{:S(2)}) collective-permute-start(bf16[2,512,128]{1,2,0:T(8,128)(2,1)S(1)} %collective-permute-done.10), channel_id=1, source_target_pairs={{0,4},{1,5},{2,6},{3,7},{4,0},{5,1},{6,2},{7,3},{8,12},{9,13},{10,... | collective-permute-start | bytes 786440 | tf_op jit(solution)/shard_map/ppermute | solution.py:12
Sparse Core Ops, SparseCore 0:
  142.3 33.6 all-reduce.2
Sparse Core Ops, SparseCore 1:
  158.7 76.6 reduce-scatter.3
